TPU v7x, 128 devices: a whole 4x4x4 slice. The times are simulated.
128 devices in a mesh: grp: 4 (over x), dev: 32 (over y, z, core).
Axes of the slice: x: 4, y: 4, z: 4, core: 2. Of those that a mesh axis runs over, the one named last changes fastest.
Arguments:
- queries: bfloat16 [32768, 4096], P(('grp', 'dev')), may hold values from -500 to 500
- new_kv: bfloat16 [32768, 2048], P(('grp', 'dev')), may hold values from -6 to 6
- kv_pool: bfloat16 [8192, 16, 2048], P(('grp', 'dev')), may hold values from -6 to 6
- hit_holder: int32 [128, 96], P(('grp', 'dev')), may hold values from 0 to 127, as said below
- hit_block: int32 [128, 96], P(('grp', 'dev')), may hold values from 0 to 63
- hit_count: int32 [128], P(('grp', 'dev')), may hold values from 48 to 96
- ssm_input: bfloat16 [32768, 8192], P(('grp', 'dev')), may hold values from -6 to 6
- step_size: float32 [32768, 128], P(('grp', 'dev')), may hold values from 0.04 to 0.16
- decay_rate: float32 [128], replicated, may hold values from 0.01 to 0.4
- state_in: float32 [32768, 16], P(('grp', 'dev')), may hold values from -6 to 6
- state_out: float32 [32768, 16], P(('grp', 'dev')), may hold values from -6 to 6
- skip_gain: float32 [128], replicated, may hold values from 0.1 to 1.9
- state_pool: float32 [256, 16, 8192], P(('grp', 'dev')), may hold values from -3 to 3
- state_group: int32 [128], P(('grp', 'dev')), may hold values from 0 to 3
- state_slot: int32 [128], P(('grp', 'dev')), may hold values from 0 to 1
Outputs:
- attended: bfloat16 [32768, 4096], P(('grp', 'dev'))
- mixed: bfloat16 [32768, 8192], P(('grp', 'dev'))
Inputs may be any that keep to these rules, and one draw needn't show every extreme that they name: `hit_holder`: the first hit_count entries of a row name different holder devices.
All inputs are finite; a program needn't handle non-finite values.
Results may differ from a plain program's by a relative error of at most 0.0027.
Values may be sent and summed in bfloat16 or wider, within the bound.
A program may use at most 256 MiB of HBM per device.

v0:
```python
import jax
import jax.numpy as jnp
from jax import lax
from jax.experimental import pallas as pl
from jax.experimental.pallas import tpu as pltpu
from jax.sharding import PartitionSpec as P

KV_HEADS = 8
HEAD_DIM = 128
SSM_HEAD_DIM = 64
BLK = 16
MIX_BLOCK = 512
AHEAD = 3
MESH = pl.DeviceIdType.MESH
N_ALL = 128
F32 = jnp.float32
BF16 = jnp.bfloat16


def place():
    g = lax.axis_index("grp")
    d = lax.axis_index("dev")
    return g, d // 8, (d // 2) % 4, d % 2


def shifted(i):
    a, b, c = i % 4, (i // 4) % 4, (i // 16) % 4
    return a, a + b, a + c, i // 64


def partner(i):
    g, y, z, core = place()
    a, b, c, e = shifted(i)
    return (g + a) % 4, (((y + b) % 4) * 4 + (z + c) % 4) * 2 + (core + e) % 2


def split(values):
    high = values.astype(BF16)
    return high, (values - high.astype(F32)).astype(BF16)


def exact_dot(a, b, dims):
    return lax.dot_general(
        a, b, (dims, ((), ())), precision=lax.Precision.HIGHEST, preferred_element_type=F32
    )


def dot(a, b, dims=((1,), (0,))):
    return lax.dot_general(a, b, (dims, ((), ())), preferred_element_type=F32)


def kernel(
    codes,
    own,
    wanted,
    steps,
    decay,
    in_map,
    out_map,
    skip,
    queries_hbm,
    new_hbm,
    pool_hbm,
    inputs_hbm,
    states_hbm,
    attended_hbm,
    mixed_hbm,
    pool,
    states,
    queries,
    new,
    inputs,
    staged,
    arrived,
    state_out,
    state_in,
    attended,
    mixed,
    bias,
    rise_pair,
    fall_pair,
    skip_pair,
    inter_high,
    inter_low,
    out_pair,
    load_sem,
    send_sem,
    recv_sem,
    state_send_sem,
    state_recv_sem,
    out_sem,
):
    g, y, z, core = place()
    dev = lax.axis_index("dev")
    me = g * 32 + dev
    loads = [
        pltpu.make_async_copy(source, target, load_sem.at[n])
        for n, (source, target) in enumerate(
            (
                (states_hbm, states),
                (pool_hbm, pool),
                (inputs_hbm, inputs),
                (queries_hbm, queries),
                (new_hbm, new),
            )
        )
    ]
    for load in loads:
        load.start()

    barrier = pltpu.get_barrier_semaphore()

    def greet(i, carry):
        pl.semaphore_signal(barrier, inc=1, device_id=partner(i), device_id_type=MESH)
        return carry

    lax.fori_loop(1, N_ALL, greet, 0)

    loads[0].wait()
    for k in range(1, 4):
        slot = jnp.maximum(codes[((g + k) % 4) * 32 + dev] // 128 - 1, 0)
        state_out[k - 1] = states[slot].astype(BF16)
    state_in[3] = states[jnp.maximum(codes[me] // 128 - 1, 0)].astype(BF16)
    loads[1].wait()

    def stage(i, carry):
        pg, pd = partner(i)
        block = pool[jnp.clip(codes[pg * 32 + pd] % 128 - 1, 0, 63)]
        for c in range(KV_HEADS):
            staged[c, i - 1, :, :HEAD_DIM] = block[:, c * HEAD_DIM : (c + 1) * HEAD_DIM]
            staged[c, i - 1, :, HEAD_DIM:] = block[:, (8 + c) * HEAD_DIM : (9 + c) * HEAD_DIM]
        return carry

    lax.fori_loop(1, N_ALL, stage, 0)
    block = pool[jnp.clip(codes[me] % 128 - 1, 0, 63)]
    for c in range(KV_HEADS):
        arrived[c, 127, :, :HEAD_DIM] = block[:, c * HEAD_DIM : (c + 1) * HEAD_DIM]
        arrived[c, 127, :, HEAD_DIM:] = block[:, (8 + c) * HEAD_DIM : (9 + c) * HEAD_DIM]

    pl.semaphore_wait(barrier, N_ALL - 1)

    for k in range(1, 4):
        pltpu.make_async_remote_copy(
            state_out.at[k - 1],
            state_in.at[k - 1],
            state_send_sem,
            state_recv_sem,
            device_id=((g + k) % 4, dev),
            device_id_type=MESH,
        ).start()

    def send(c):
        def one(i, carry):
            pltpu.make_async_remote_copy(
                staged.at[c, i - 1],
                arrived.at[c, i - 1],
                send_sem.at[c],
                recv_sem.at[c],
                device_id=partner(i),
                device_id_type=MESH,
            ).start()
            return carry

        lax.fori_loop(1, N_ALL, one, 0)

    for c in range(AHEAD):
        send(c)

    suffix = steps.shape[0]
    rows = lax.broadcasted_iota(jnp.int32, (suffix, suffix), 0)
    lower = rows >= lax.broadcasted_iota(jnp.int32, (suffix, suffix), 1)
    total = exact_dot(jnp.where(lower, 1.0, 0.0), steps[...] * decay[...], ((1,), (0,)))
    heads = total.shape[1]
    high, low = split(jnp.exp(-total))
    rise_pair[:, :heads] = high
    rise_pair[:, heads:] = low
    high, low = split(jnp.exp(total) * steps[...])
    fall_pair[:, :heads] = high
    fall_pair[:, heads:] = low
    high, low = split(jnp.broadcast_to(skip[...], (16, heads)))
    skip_pair[:, :heads] = high
    skip_pair[:, heads:] = low
    inter = jnp.where(lower, exact_dot(out_map[...], in_map[...], ((1,), (1,))), 0.0)
    high, low = split(inter)
    inter_high[...] = high
    inter_low[...] = low
    high, low = split(out_map[...])
    out_pair[...] = jnp.concatenate([high, low], axis=1)

    holder = lax.broadcasted_iota(jnp.int32, (N_ALL, N_ALL * BLK), 0)
    offset = lax.broadcasted_iota(jnp.int32, (N_ALL, N_ALL * BLK), 1) // BLK + 1
    a, b, c, e = shifted(offset % N_ALL)
    source = ((g + 8 - a) % 4) * 32 + ((y + 8 - b) % 4) * 8 + ((z + 8 - c) % 4) * 2 + (core + e) % 2
    chosen = jnp.where(holder == source, 1.0, 0.0).astype(BF16)
    live = jnp.where(wanted[...] >= 0, 1.0, 0.0).astype(BF16)
    seen = dot(jnp.broadcast_to(live, (16, N_ALL)), chosen)
    bias[...] = jnp.where(seen[:8] > 0.5, 0.0, -1e30)

    pltpu.make_async_copy(state_out, state_in.at[0:3], state_recv_sem).wait()
    loads[2].wait()
    which = (g - own[0] + 7) % 4

    def mix(j, carry):
        columns = pl.ds(pl.multiple_of(j * MIX_BLOCK, MIX_BLOCK), MIX_BLOCK)
        row = lax.broadcasted_iota(jnp.int32, (2 * heads, MIX_BLOCK), 0) % heads
        head = (lax.broadcasted_iota(jnp.int32, (2 * heads, MIX_BLOCK), 1) + j * MIX_BLOCK) // SSM_HEAD_DIM
        spread = jnp.where(row == head, 1.0, 0.0).astype(BF16)
        values = inputs[:, columns].astype(F32)
        high, low = split(dot(fall_pair[...], spread) * values)
        start = state_in[which, :, columns]
        inner = dot(inter_high[...], high) + dot(inter_low[...], high) + dot(inter_high[...], low)
        inner = inner + dot(out_pair[...], jnp.concatenate([start, start], axis=0))
        result = dot(rise_pair[...], spread) * inner + dot(skip_pair[...], spread)[:1] * values
        mixed[:, columns] = result.astype(BF16)
        return carry

    lax.fori_loop(0, inputs.shape[1] // MIX_BLOCK, mix, 0)
    store_mixed = pltpu.make_async_copy(mixed, mixed_hbm, out_sem.at[0])
    store_mixed.start()

    loads[3].wait()
    loads[4].wait()
    group = queries.shape[1] // (KV_HEADS * HEAD_DIM)
    scale = HEAD_DIM ** (-0.5)
    width = group * HEAD_DIM

    def store_of(c):
        columns = pl.ds(pl.multiple_of(c * width, width), width)
        return pltpu.make_async_copy(
            attended.at[:, columns], attended_hbm.at[:, columns], out_sem.at[1]
        )

    def attend(c, carry):
        pltpu.make_async_copy(
            staged.at[c, 0 : N_ALL - 1], arrived.at[c, 0 : N_ALL - 1], recv_sem.at[c]
        ).wait()
        keys = arrived[c, :, :, :HEAD_DIM].reshape(N_ALL * BLK, HEAD_DIM)
        values = arrived[c, :, :, HEAD_DIM:].reshape(N_ALL * BLK, HEAD_DIM)
        keys_new = new[:, pl.ds(pl.multiple_of(c * HEAD_DIM, HEAD_DIM), HEAD_DIM)]
        values_new = new[:, pl.ds(pl.multiple_of((c + 8) * HEAD_DIM, HEAD_DIM), HEAD_DIM)]

        def one(h, carry):
            columns = pl.ds(pl.multiple_of((c * group + h) * HEAD_DIM, HEAD_DIM), HEAD_DIM)
            query = queries[:, columns]
            old = dot(query, keys, ((1,), (1,))) * scale + bias[0:1]
            fresh = jnp.where(lower, dot(query, keys_new, ((1,), (1,))) * scale, -1e30)
            peak = jnp.maximum(
                jnp.max(old, axis=1, keepdims=True), jnp.max(fresh, axis=1, keepdims=True)
            )
            old = jnp.exp(old - peak)
            fresh = jnp.exp(fresh - peak)
            weight = jnp.sum(old, axis=1, keepdims=True) + jnp.sum(fresh, axis=1, keepdims=True)
            result = dot(old.astype(BF16), values) + dot(fresh.astype(BF16), values_new)
            attended[:, columns] = (result / weight).astype(BF16)
            return carry

        lax.fori_loop(0, group, one, 0)
        store_of(c).start()

        @pl.when(c + AHEAD < KV_HEADS)
        def _():
            send(c + AHEAD)

        return carry

    lax.fori_loop(0, KV_HEADS, attend, 0)

    pltpu.make_async_copy(attended, attended_hbm, out_sem.at[1]).wait()
    store_mixed.wait()
    pltpu.make_async_copy(state_out, state_in.at[0:3], state_send_sem).wait()
    for c in range(KV_HEADS):
        pltpu.make_async_copy(
            staged.at[c, 0 : N_ALL - 1], arrived.at[c, 0 : N_ALL - 1], send_sem.at[c]
        ).wait()


def body(
    queries,
    new_kv,
    kv_pool,
    hit_holder,
    hit_block,
    hit_count,
    ssm_input,
    step_size,
    decay_rate,
    state_in,
    state_out,
    skip_gain,
    state_pool,
    state_group,
    state_slot,
):
    n_all = lax.axis_size(("grp", "dev"))
    n_dev = lax.axis_size("dev")
    holders = jnp.arange(n_all, dtype=jnp.int32)
    entries = jnp.arange(hit_holder.shape[1], dtype=jnp.int32)
    chosen = (hit_holder[0][:, None] == holders[None, :]) & (entries[:, None] < hit_count[0])
    wanted = jnp.sum(jnp.where(chosen, hit_block[0][:, None] + 1, 0), axis=0) - 1
    state_holder = state_group[0] * n_dev + lax.axis_index("dev")
    asked_state = jnp.where(holders == state_holder, state_slot[0] + 1, 0)
    codes = lax.all_to_all(
        (wanted + 1 + 128 * asked_state).reshape(n_all, 1),
        ("grp", "dev"),
        split_axis=0,
        concat_axis=0,
        tiled=True,
    )[:, 0]

    suffix, channels = ssm_input.shape
    heads = decay_rate.shape[0]
    states = state_in.shape[1]
    smem = pl.BlockSpec(memory_space=pltpu.SMEM)
    vmem = pl.BlockSpec(memory_space=pltpu.VMEM)
    left = pl.BlockSpec(memory_space=pl.ANY)
    return pl.pallas_call(
        kernel,
        name="prefill",
        out_shape=(
            jax.ShapeDtypeStruct(queries.shape, BF16),
            jax.ShapeDtypeStruct(ssm_input.shape, BF16),
        ),
        in_specs=[smem] * 2 + [vmem] * 6 + [left] * 5,
        out_specs=(left, left),
        scratch_shapes=[
            pltpu.VMEM(kv_pool.shape, BF16),
            pltpu.VMEM(state_pool.shape, F32),
            pltpu.VMEM(queries.shape, BF16),
            pltpu.VMEM(new_kv.shape, BF16),
            pltpu.VMEM(ssm_input.shape, BF16),
            pltpu.VMEM((KV_HEADS, n_all, BLK, 2 * HEAD_DIM), BF16),
            pltpu.VMEM((KV_HEADS, n_all, BLK, 2 * HEAD_DIM), BF16),
            pltpu.VMEM((3, states, channels), BF16),
            pltpu.VMEM((4, states, channels), BF16),
            pltpu.VMEM(queries.shape, BF16),
            pltpu.VMEM(ssm_input.shape, BF16),
            pltpu.VMEM((8, n_all * BLK), F32),
            pltpu.VMEM((suffix, 2 * heads), BF16),
            pltpu.VMEM((suffix, 2 * heads), BF16),
            pltpu.VMEM((16, 2 * heads), BF16),
            pltpu.VMEM((suffix, suffix), BF16),
            pltpu.VMEM((suffix, suffix), BF16),
            pltpu.VMEM((suffix, 2 * states), BF16),
            pltpu.SemaphoreType.DMA((5,)),
            pltpu.SemaphoreType.DMA((KV_HEADS,)),
            pltpu.SemaphoreType.DMA((KV_HEADS,)),
            pltpu.SemaphoreType.DMA,
            pltpu.SemaphoreType.DMA,
            pltpu.SemaphoreType.DMA((2,)),
        ],
        compiler_params=pltpu.CompilerParams(
            collective_id=0, has_side_effects=True, vmem_limit_bytes=63 * 2**20
        ),
    )(
        codes,
        state_group,
        wanted[None, :],
        step_size,
        decay_rate[None, :],
        state_in,
        state_out,
        skip_gain[None, :],
        queries,
        new_kv,
        kv_pool,
        ssm_input,
        state_pool,
    )


def solution(mesh):
    return jax.shard_map(
        body,
        mesh=mesh,
        in_specs=(
            P(("grp", "dev"), None),
            P(("grp", "dev"), None),
            P(("grp", "dev"), None, None),
            P(("grp", "dev"), None),
            P(("grp", "dev"), None),
            P(("grp", "dev")),
            P(("grp", "dev"), None),
            P(("grp", "dev"), None),
            P(),
            P(("grp", "dev"), None),
            P(("grp", "dev"), None),
            P(),
            P(("grp", "dev"), None, None),
            P(("grp", "dev")),
            P(("grp", "dev")),
        ),
        out_specs=(P(("grp", "dev"), None), P(("grp", "dev"), None)),
        check_vma=False,
    )
```

profile of v0, /device:TPU:1, one launch (start us, length us, event | category | flops | bytes accessed | tf_op | source)
XLA Modules:
  0.0 157.0 jit_solution(1903920917921136782)
XLA Ops:
  2.6 0.7 add_bitcast_fusion.1
  3.2 0.8 select_reduce_fusion
  4.0 0.7 copy.25
  4.8 11.5 %all-to-all-start = ((s32[128,1,1]{2,1,0:T(1,128)}), s32[128,1,1]{2,1,0:T(1,128)S(1)}, u32[]{:S(2)}, u32[]{:S(2)}) async-start(s32[128,1,1]{2,1,0:T(1,128)} %copy.25), calls=%async_computation | async-start | bytes 131072 | tf_op jit(solution)/shard_map/all_to_all | solution.py:302
  16.3 0.5 add_bitcast_fusion.wanted
  16.8 1.5 copy.26.in_map
  18.2 1.5 copy.27.out_map
  19.7 5.9 %all-to-all-done = s32[128,1,1]{2,1,0:T(1,128)S(1)} async-done(((s32[128,1,1]{2,1,0:T(1,128)}), s32[128,1,1]{2,1,0:T(1,128)S(1)}, u32[]{:S(2)}, u32[]{:S(2)}) %all-to-all-start) | async-done | bytes 544 | tf_op jit(solution)/shard_map/all_to_all | solution.py:302
  25.6 2.9 %reduce.codes = s32[128]{0:T(128)} reduce(s32[128,1,1]{2,1,0:T(1,128)S(1)} %all-to-all-done, s32[]{:T(128)} %constant.5.clone.1), dimensions={1,2}, to_apply=%all_to_all.4.reduce_sub_computation | reduce | bytes 1028 | tf_op jit(solution)/shard_map/all_to_all | solution.py:302
  28.5 123.2 %prefill.1 = (bf16[256,4096]{1,0:T(8,128)(2,1)}, bf16[256,8192]{1,0:T(8,128)(2,1)}) custom-call(s32[128]{0:T(128)} %reduce.codes, s32[1]{0:T(128)S(6)} %copy.31.own, s32[1,128]{1,0:T(1,128)} %add_bitcast_fusion.wanted, f32[256,128]{1,0:T(8,128)} %steps.1, f32[1,128]{1,0:T(1,128)} %bitcast.13, f32[256,16]{1,0:T(8,128)} %copy.26.in_map, ...), custom_call_target="tpu_custom_call" | custom-call | tf_op jit(solution)/shard_map/prefill/pallas_call | solution.py:316
  151.7 0.0 copy-start
  151.7 3.3 %copy.33 = bf16[256,4096]{1,0:T(8,128)(2,1)} copy(bf16[256,4096]{1,0:T(8,128)(2,1)} %get-tuple-element.4) | data formatting | bytes 4194304
  155.0 0.0 copy-done
  155.0 2.0 %copy.34 = bf16[256,8192]{1,0:T(8,128)(2,1)} copy(bf16[256,8192]{1,0:T(8,128)(2,1)S(1)} %copy-done) | data formatting | bytes 8388608
  (2 shorter events, 0.0 us)
Async XLA Ops:
  4.8 20.9 %all-to-all-start = ((s32[128,1,1]{2,1,0:T(1,128)}), s32[128,1,1]{2,1,0:T(1,128)S(1)}, u32[]{:S(2)}, u32[]{:S(2)}) async-start(s32[128,1,1]{2,1,0:T(1,128)} %copy.25), calls=%async_computation | async-start | bytes 131072 | tf_op jit(solution)/shard_map/all_to_all | solution.py:302
  151.7 3.3 %copy-start = (bf16[256,8192]{1,0:T(8,128)(2,1)S(1)}, bf16[256,8192]{1,0:T(8,128)(2,1)}, u32[]{:S(2)}) copy-start(bf16[256,8192]{1,0:T(8,128)(2,1)} %get-tuple-element.5) | copy-start | bytes 12582916
where the time goes:
time: 157 us
  Pallas kernels  123 us (78%)
  starting transfers between devices  11.5 us (7%)
  local copies, waits for them, and re-layouts  8.97 us (6%)
  waiting for transfers between devices  5.92 us (4%)
  other arithmetic  4.86 us (3%)
  between operations  2.61 us (2%)
    pallas_call x1, Pallas kernels, body(): pl.pallas_call(kernel, name='prefill', out_shape=(jax.ShapeDtypeStruct(qu...  123 us
    all_to_all x1, starting transfers between devices, body(): lax.all_to_all((wanted + 1 + 128 * asked_state).reshape(n_all, 1), ('grp'...  11.5 us
    unnamed x6, local copies, waits for them, and re-layouts  8.24 us
    all_to_all x1, waiting for transfers between devices, body(): lax.all_to_all((wanted + 1 + 128 * asked_state).reshape(n_all, 1), ('grp'...  5.92 us
  transfers between devices with their start and end apart: 1, of which 1 were waited for; matrix products, arithmetic and copies ran while one was open for 2% of the time, Pallas kernels for 0%

commit v1 on v0

--- a/solution.py
+++ b/solution.py
@@ -11,6 +11,7 @@
 BLK = 16
 MIX_BLOCK = 512
 AHEAD = 3
+VMEM_LIMIT = 48 * 2**20
 MESH = pl.DeviceIdType.MESH
 N_ALL = 128
 F32 = jnp.float32
@@ -20,18 +21,27 @@
 def place():
     g = lax.axis_index("grp")
     d = lax.axis_index("dev")
-    return g, d // 8, (d // 2) % 4, d % 2
+    return g, lax.div(d, 8), lax.rem(lax.div(d, 2), 4), lax.rem(d, 2)
 
 
 def shifted(i):
-    a, b, c = i % 4, (i // 4) % 4, (i // 16) % 4
-    return a, a + b, a + c, i // 64
+    a, b, c = lax.rem(i, 4), lax.rem(lax.div(i, 4), 4), lax.rem(lax.div(i, 16), 4)
+    return a, lax.rem(a + b, 4), lax.rem(a + c, 4), lax.div(i, 64)
+
+
+def at(a, b, c, e):
+    g, y, z, core = place()
+    dev = (lax.rem(y + b, 4) * 4 + lax.rem(z + c, 4)) * 2 + lax.rem(core + e, 2)
+    return lax.rem(g + a, 4), dev
 
 
 def partner(i):
-    g, y, z, core = place()
-    a, b, c, e = shifted(i)
-    return (g + a) % 4, (((y + b) % 4) * 4 + (z + c) % 4) * 2 + (core + e) % 2
+    return at(*shifted(i))
+
+
+def gathered_row(a, b, c, e):
+    back_a, back_b, back_c = lax.rem(4 - a, 4), lax.rem(4 - b, 4), lax.rem(4 - c, 4)
+    return (back_b * 4 + back_c) * 8 + back_a * 2 + e
 
 
 def split(values):
@@ -50,9 +60,11 @@
 
 
 def kernel(
-    codes,
-    own,
-    wanted,
+    state_group,
+    state_slot,
+    hit_count,
+    hit_holder,
+    hit_block,
     steps,
     decay,
     in_map,
@@ -63,8 +75,8 @@
     pool_hbm,
     inputs_hbm,
     states_hbm,
-    attended_hbm,
-    mixed_hbm,
+    attended,
+    mixed,
     pool,
     states,
     queries,
@@ -74,8 +86,9 @@
     arrived,
     state_out,
     state_in,
-    attended,
-    mixed,
+    asked,
+    asked_near,
+    asked_all,
     bias,
     rise_pair,
     fall_pair,
@@ -88,7 +101,9 @@
     recv_sem,
     state_send_sem,
     state_recv_sem,
-    out_sem,
+    ask_send_sem,
+    ask_recv_sem,
+    ask_sem,
 ):
     g, y, z, core = place()
     dev = lax.axis_index("dev")
@@ -109,45 +124,88 @@
         load.start()
 
     barrier = pltpu.get_barrier_semaphore()
-
-    def greet(i, carry):
-        pl.semaphore_signal(barrier, inc=1, device_id=partner(i), device_id_type=MESH)
-        return carry
-
-    lax.fori_loop(1, N_ALL, greet, 0)
-
+    near = [(a, e) for a in (2, 1, 3, 0) for e in (1, 0) if (a, e) != (0, 0)]
+    plane = [(b, c) for b in (2, 1, 3, 0) for c in (2, 1, 3, 0) if (b, c) != (0, 0)]
+    for offset in [(a, 0, 0, e) for a, e in near] + [(0, b, c, 0) for b, c in plane]:
+        pl.semaphore_signal(barrier, inc=1, device_id=at(*offset), device_id_type=MESH)
+
+    entries = hit_holder.shape[1]
+    entry = lax.broadcasted_iota(jnp.int32, (1, entries), 1)
+    holder = jnp.where(entry < hit_count[0], hit_holder[...], -1)
+    held = lax.broadcasted_iota(jnp.int32, (N_ALL, entries), 0) == holder
+    numbers = jnp.broadcast_to((hit_block[...] + 1).astype(F32), (8, entries))
+    wanted = exact_dot(numbers, jnp.where(held, 1.0, 0.0), ((1,), (1,)))[:1]
+    lane = lax.broadcasted_iota(jnp.int32, (1, N_ALL), 1)
+    asked_state = jnp.where(lane == state_group[0] * 32 + dev, state_slot[0] + 1, 0)
+    asked[0] = (wanted + 0.5).astype(jnp.int32) + 128 * asked_state
+
+    pl.semaphore_wait(barrier, len(near) + len(plane))
+    for a, e in near:
+        pltpu.make_async_remote_copy(
+            asked.at[pl.ds(0, 1)],
+            asked.at[pl.ds(a * 2 + e, 1)],
+            ask_send_sem.at[0],
+            ask_recv_sem.at[0],
+            device_id=at(a, 0, 0, e),
+            device_id_type=MESH,
+        ).start()
+    first = pltpu.make_async_copy(asked.at[pl.ds(0, 7)], asked.at[pl.ds(1, 7)], ask_recv_sem.at[0])
+    first.wait()
+    for b, c in plane:
+        pltpu.make_async_remote_copy(
+            asked.at[pl.ds(0, 8)],
+            asked.at[pl.ds((b * 4 + c) * 8, 8)],
+            ask_send_sem.at[1],
+            ask_recv_sem.at[1],
+            device_id=at(0, b, c, 0),
+            device_id_type=MESH,
+        ).start()
+
+    copy_near = pltpu.make_async_copy(asked.at[pl.ds(0, 8)], asked_near, ask_sem)
+    copy_near.start()
+    copy_near.wait()
     loads[0].wait()
+
+    def slot_for(row):
+        return jnp.clip(lax.div(asked_near[row, 0, me], 128) - 1, 0, 1)
+
     for k in range(1, 4):
-        slot = jnp.maximum(codes[((g + k) % 4) * 32 + dev] // 128 - 1, 0)
-        state_out[k - 1] = states[slot].astype(BF16)
-    state_in[3] = states[jnp.maximum(codes[me] // 128 - 1, 0)].astype(BF16)
-    loads[1].wait()
-
-    def stage(i, carry):
-        pg, pd = partner(i)
-        block = pool[jnp.clip(codes[pg * 32 + pd] % 128 - 1, 0, 63)]
-        for c in range(KV_HEADS):
-            staged[c, i - 1, :, :HEAD_DIM] = block[:, c * HEAD_DIM : (c + 1) * HEAD_DIM]
-            staged[c, i - 1, :, HEAD_DIM:] = block[:, (8 + c) * HEAD_DIM : (9 + c) * HEAD_DIM]
-        return carry
-
-    lax.fori_loop(1, N_ALL, stage, 0)
-    block = pool[jnp.clip(codes[me] % 128 - 1, 0, 63)]
-    for c in range(KV_HEADS):
-        arrived[c, 127, :, :HEAD_DIM] = block[:, c * HEAD_DIM : (c + 1) * HEAD_DIM]
-        arrived[c, 127, :, HEAD_DIM:] = block[:, (8 + c) * HEAD_DIM : (9 + c) * HEAD_DIM]
-
-    pl.semaphore_wait(barrier, N_ALL - 1)
-
+        state_out[k - 1] = states[slot_for(gathered_row(k, 0, 0, 0))].astype(BF16)
+    state_in[3] = states[slot_for(0)].astype(BF16)
     for k in range(1, 4):
         pltpu.make_async_remote_copy(
             state_out.at[k - 1],
             state_in.at[k - 1],
             state_send_sem,
             state_recv_sem,
-            device_id=((g + k) % 4, dev),
+            device_id=at(k, 0, 0, 0),
             device_id_type=MESH,
         ).start()
+
+    second = pltpu.make_async_copy(
+        asked.at[pl.ds(0, 120)], asked.at[pl.ds(8, 120)], ask_recv_sem.at[1]
+    )
+    second.wait()
+    copy_all = pltpu.make_async_copy(asked, asked_all, ask_sem)
+    copy_all.start()
+    copy_all.wait()
+    loads[1].wait()
+
+    def block_for(row):
+        return jnp.clip(lax.rem(asked_all[row, 0, me], 128) - 1, 0, 63)
+
+    def stage(i, carry):
+        block = pool[block_for(gathered_row(*shifted(i)))]
+        for c in range(KV_HEADS):
+            staged[c, i - 1, :, :HEAD_DIM] = block[:, c * HEAD_DIM : (c + 1) * HEAD_DIM]
+            staged[c, i - 1, :, HEAD_DIM:] = block[:, (8 + c) * HEAD_DIM : (9 + c) * HEAD_DIM]
+        return carry
+
+    lax.fori_loop(1, N_ALL, stage, 0)
+    block = pool[block_for(0)]
+    for c in range(KV_HEADS):
+        arrived[c, 127, :, :HEAD_DIM] = block[:, c * HEAD_DIM : (c + 1) * HEAD_DIM]
+        arrived[c, 127, :, HEAD_DIM:] = block[:, (8 + c) * HEAD_DIM : (9 + c) * HEAD_DIM]
 
     def send(c):
         def one(i, carry):
@@ -180,25 +238,25 @@
     high, low = split(jnp.broadcast_to(skip[...], (16, heads)))
     skip_pair[:, :heads] = high
     skip_pair[:, heads:] = low
-    inter = jnp.where(lower, exact_dot(out_map[...], in_map[...], ((1,), (1,))), 0.0)
+    inter = jnp.where(lower, exact_dot(out_map[...], in_map[...], ((0,), (0,))), 0.0)
     high, low = split(inter)
     inter_high[...] = high
     inter_low[...] = low
     high, low = split(out_map[...])
-    out_pair[...] = jnp.concatenate([high, low], axis=1)
+    out_pair[...] = jnp.concatenate([high, low], axis=0)
 
     holder = lax.broadcasted_iota(jnp.int32, (N_ALL, N_ALL * BLK), 0)
     offset = lax.broadcasted_iota(jnp.int32, (N_ALL, N_ALL * BLK), 1) // BLK + 1
     a, b, c, e = shifted(offset % N_ALL)
-    source = ((g + 8 - a) % 4) * 32 + ((y + 8 - b) % 4) * 8 + ((z + 8 - c) % 4) * 2 + (core + e) % 2
+    source = ((g + 4 - a) % 4) * 32 + ((y + 4 - b) % 4) * 8 + ((z + 4 - c) % 4) * 2 + (core + e) % 2
     chosen = jnp.where(holder == source, 1.0, 0.0).astype(BF16)
-    live = jnp.where(wanted[...] >= 0, 1.0, 0.0).astype(BF16)
+    live = jnp.where(wanted > 0.5, 1.0, 0.0).astype(BF16)
     seen = dot(jnp.broadcast_to(live, (16, N_ALL)), chosen)
     bias[...] = jnp.where(seen[:8] > 0.5, 0.0, -1e30)
 
     pltpu.make_async_copy(state_out, state_in.at[0:3], state_recv_sem).wait()
     loads[2].wait()
-    which = (g - own[0] + 7) % 4
+    which = lax.rem(g - state_group[0] + 7, 4)
 
     def mix(j, carry):
         columns = pl.ds(pl.multiple_of(j * MIX_BLOCK, MIX_BLOCK), MIX_BLOCK)
@@ -209,26 +267,17 @@
         high, low = split(dot(fall_pair[...], spread) * values)
         start = state_in[which, :, columns]
         inner = dot(inter_high[...], high) + dot(inter_low[...], high) + dot(inter_high[...], low)
-        inner = inner + dot(out_pair[...], jnp.concatenate([start, start], axis=0))
+        inner = inner + dot(out_pair[...], jnp.concatenate([start, start], axis=0), ((0,), (0,)))
         result = dot(rise_pair[...], spread) * inner + dot(skip_pair[...], spread)[:1] * values
         mixed[:, columns] = result.astype(BF16)
         return carry
 
     lax.fori_loop(0, inputs.shape[1] // MIX_BLOCK, mix, 0)
-    store_mixed = pltpu.make_async_copy(mixed, mixed_hbm, out_sem.at[0])
-    store_mixed.start()
 
     loads[3].wait()
     loads[4].wait()
     group = queries.shape[1] // (KV_HEADS * HEAD_DIM)
     scale = HEAD_DIM ** (-0.5)
-    width = group * HEAD_DIM
-
-    def store_of(c):
-        columns = pl.ds(pl.multiple_of(c * width, width), width)
-        return pltpu.make_async_copy(
-            attended.at[:, columns], attended_hbm.at[:, columns], out_sem.at[1]
-        )
 
     def attend(c, carry):
         pltpu.make_async_copy(
@@ -255,7 +304,6 @@
             return carry
 
         lax.fori_loop(0, group, one, 0)
-        store_of(c).start()
 
         @pl.when(c + AHEAD < KV_HEADS)
         def _():
@@ -265,8 +313,10 @@
 
     lax.fori_loop(0, KV_HEADS, attend, 0)
 
-    pltpu.make_async_copy(attended, attended_hbm, out_sem.at[1]).wait()
-    store_mixed.wait()
+    pltpu.make_async_copy(asked.at[pl.ds(0, 7)], asked.at[pl.ds(1, 7)], ask_send_sem.at[0]).wait()
+    pltpu.make_async_copy(
+        asked.at[pl.ds(0, 120)], asked.at[pl.ds(8, 120)], ask_send_sem.at[1]
+    ).wait()
     pltpu.make_async_copy(state_out, state_in.at[0:3], state_send_sem).wait()
     for c in range(KV_HEADS):
         pltpu.make_async_copy(
@@ -292,21 +342,6 @@
     state_slot,
 ):
     n_all = lax.axis_size(("grp", "dev"))
-    n_dev = lax.axis_size("dev")
-    holders = jnp.arange(n_all, dtype=jnp.int32)
-    entries = jnp.arange(hit_holder.shape[1], dtype=jnp.int32)
-    chosen = (hit_holder[0][:, None] == holders[None, :]) & (entries[:, None] < hit_count[0])
-    wanted = jnp.sum(jnp.where(chosen, hit_block[0][:, None] + 1, 0), axis=0) - 1
-    state_holder = state_group[0] * n_dev + lax.axis_index("dev")
-    asked_state = jnp.where(holders == state_holder, state_slot[0] + 1, 0)
-    codes = lax.all_to_all(
-        (wanted + 1 + 128 * asked_state).reshape(n_all, 1),
-        ("grp", "dev"),
-        split_axis=0,
-        concat_axis=0,
-        tiled=True,
-    )[:, 0]
-
     suffix, channels = ssm_input.shape
     heads = decay_rate.shape[0]
     states = state_in.shape[1]
@@ -317,11 +352,11 @@
         kernel,
         name="prefill",
         out_shape=(
-            jax.ShapeDtypeStruct(queries.shape, BF16),
-            jax.ShapeDtypeStruct(ssm_input.shape, BF16),
+            pltpu.VMEM(queries.shape, BF16),
+            pltpu.VMEM(ssm_input.shape, BF16),
         ),
-        in_specs=[smem] * 2 + [vmem] * 6 + [left] * 5,
-        out_specs=(left, left),
+        in_specs=[smem] * 3 + [vmem] * 7 + [left] * 5,
+        out_specs=(vmem, vmem),
         scratch_shapes=[
             pltpu.VMEM(kv_pool.shape, BF16),
             pltpu.VMEM(state_pool.shape, F32),
@@ -332,33 +367,38 @@
             pltpu.VMEM((KV_HEADS, n_all, BLK, 2 * HEAD_DIM), BF16),
             pltpu.VMEM((3, states, channels), BF16),
             pltpu.VMEM((4, states, channels), BF16),
-            pltpu.VMEM(queries.shape, BF16),
-            pltpu.VMEM(ssm_input.shape, BF16),
+            pltpu.VMEM((n_all, 1, n_all), jnp.int32),
+            pltpu.SMEM((8, 1, n_all), jnp.int32),
+            pltpu.SMEM((n_all, 1, n_all), jnp.int32),
             pltpu.VMEM((8, n_all * BLK), F32),
             pltpu.VMEM((suffix, 2 * heads), BF16),
             pltpu.VMEM((suffix, 2 * heads), BF16),
             pltpu.VMEM((16, 2 * heads), BF16),
             pltpu.VMEM((suffix, suffix), BF16),
             pltpu.VMEM((suffix, suffix), BF16),
-            pltpu.VMEM((suffix, 2 * states), BF16),
+            pltpu.VMEM((2 * states, suffix), BF16),
             pltpu.SemaphoreType.DMA((5,)),
             pltpu.SemaphoreType.DMA((KV_HEADS,)),
             pltpu.SemaphoreType.DMA((KV_HEADS,)),
             pltpu.SemaphoreType.DMA,
             pltpu.SemaphoreType.DMA,
             pltpu.SemaphoreType.DMA((2,)),
+            pltpu.SemaphoreType.DMA((2,)),
+            pltpu.SemaphoreType.DMA,
         ],
         compiler_params=pltpu.CompilerParams(
-            collective_id=0, has_side_effects=True, vmem_limit_bytes=63 * 2**20
+            collective_id=0, has_side_effects=True, vmem_limit_bytes=VMEM_LIMIT
         ),
     )(
-        codes,
         state_group,
-        wanted[None, :],
+        state_slot,
+        hit_count,
+        hit_holder,
+        hit_block,
         step_size,
         decay_rate[None, :],
-        state_in,
-        state_out,
+        state_in.T,
+        state_out.T,
         skip_gain[None, :],
         queries,
         new_kv,

time: 157 us -> 130 us (0.83)
  starting transfers between devices: 11.5 us -> 0 us
  waiting for transfers between devices: 5.92 us -> 0 us
  local copies, waits for them, and re-layouts: 8.97 us -> 3.33 us
  other arithmetic: 4.86 us -> 0 us
    all_to_all x1 -> x0, starting transfers between devices: 11.5 us -> none  [body(): lax.all_to_all((wanted + 1 + 128 * asked_state).reshape(n_all, 1), ('grp'...]
    all_to_all x1 -> x0, waiting for transfers between devices: 5.92 us -> none  [body(): lax.all_to_all((wanted + 1 + 128 * asked_state).reshape(n_all, 1), ('grp'...]
    unnamed x6 -> x2, local copies, waits for them, and re-layouts: 8.24 us -> 3.33 us
    all_to_all x1 -> x0, other arithmetic: 2.89 us -> none  [body(): lax.all_to_all((wanted + 1 + 128 * asked_state).reshape(n_all, 1), ('grp'...]
  transfers between devices with their start and end apart: 1 -> 0, of which waited for: 1 -> 0; matrix products, arithmetic and copies ran while one was open for 2% -> 0% of each run, Pallas kernels for 0% -> 0%
where the time goes in v1:
time: 130 us
  Pallas kernels  124 us (95%)
  local copies, waits for them, and re-layouts  3.33 us (3%)
  between operations  2.58 us (2%)
    pallas_call x1, Pallas kernels, body(): pl.pallas_call(kernel, name='prefill', out_shape=(pltpu.VMEM(queries.shap...  124 us
    unnamed x2, local copies, waits for them, and re-layouts  3.33 us

profile of v1, /device:TPU:1, one launch (start us, length us, event | category | flops | bytes accessed | tf_op | source)
XLA Modules:
  0.0 129.9 jit_solution(13648259633067768042)
XLA Ops:
  2.6 124.0 %prefill.1 = (bf16[256,4096]{1,0:T(8,128)(2,1)S(1)}, bf16[256,8192]{1,0:T(8,128)(2,1)S(1)}) custom-call(s32[1]{0:T(128)S(6)} %copy.22.state_group, s32[1]{0:T(128)S(6)} %copy.23.state_slot, s32[1]{0:T(128)S(6)} %copy.21.hit_count, s32[1,96]{1,0:T(1,128)} %hit_holder.1, s32[1,96]{1,0:T(1,128)} %hit_block.1, f32[256,128]{1,0:T(8,128)} %steps.1, ...), custom_call_target="tpu_custom_call" | custom-call | tf_op jit(solution)/shard_map/prefill/pallas_call | solution.py:351
  126.6 1.3 %copy.19 = bf16[256,4096]{1,0:T(8,128)(2,1)} copy(bf16[256,4096]{1,0:T(8,128)(2,1)S(1)} %get-tuple-element.2) | data formatting | bytes 4194304
  127.9 2.0 %copy.20 = bf16[256,8192]{1,0:T(8,128)(2,1)} copy(bf16[256,8192]{1,0:T(8,128)(2,1)S(1)} %get-tuple-element.3) | data formatting | bytes 8388608

commit v2 on v1

--- a/solution.py
+++ b/solution.py
@@ -84,11 +84,15 @@
     inputs,
     staged,
     arrived,
+    staged_last,
+    arrived_last,
     state_out,
     state_in,
     asked,
-    asked_near,
     asked_all,
+    weights,
+    partial,
+    rounded,
     bias,
     rise_pair,
     fall_pair,
@@ -161,17 +165,15 @@
             device_id_type=MESH,
         ).start()
 
-    copy_near = pltpu.make_async_copy(asked.at[pl.ds(0, 8)], asked_near, ask_sem)
-    copy_near.start()
-    copy_near.wait()
     loads[0].wait()
 
-    def slot_for(row):
-        return jnp.clip(lax.div(asked_near[row, 0, me], 128) - 1, 0, 1)
+    def state_for(row):
+        code = jnp.sum(jnp.where(lane == me, asked[row], 0), axis=1, keepdims=True)
+        return jnp.where(code >= 256, states[1], states[0]).astype(BF16)
 
     for k in range(1, 4):
-        state_out[k - 1] = states[slot_for(gathered_row(k, 0, 0, 0))].astype(BF16)
-    state_in[3] = states[slot_for(0)].astype(BF16)
+        state_out[k - 1] = state_for(gathered_row(k, 0, 0, 0))
+    state_in[3] = state_for(0)
     for k in range(1, 4):
         pltpu.make_async_remote_copy(
             state_out.at[k - 1],
@@ -182,6 +184,26 @@
             device_id_type=MESH,
         ).start()
 
+    last = KV_HEADS - 1
+
+    def lay(code, blocks, blocks_last, slot):
+        block = pool[jnp.clip(lax.rem(code, 128) - 1, 0, 63)]
+        for c in range(last):
+            blocks[c, slot, :, :HEAD_DIM] = block[:, c * HEAD_DIM : (c + 1) * HEAD_DIM]
+            blocks[c, slot, :, HEAD_DIM:] = block[:, (8 + c) * HEAD_DIM : (9 + c) * HEAD_DIM]
+        blocks_last[0, slot] = block[:, last * HEAD_DIM : KV_HEADS * HEAD_DIM]
+        blocks_last[1, slot] = block[:, (8 + last) * HEAD_DIM :]
+
+    def send_one(source, target, n, i):
+        pltpu.make_async_remote_copy(
+            source.at[i - 1],
+            target.at[i - 1],
+            send_sem.at[n],
+            recv_sem.at[n],
+            device_id=partner(i),
+            device_id_type=MESH,
+        ).start()
+
     second = pltpu.make_async_copy(
         asked.at[pl.ds(0, 120)], asked.at[pl.ds(8, 120)], ask_recv_sem.at[1]
     )
@@ -191,38 +213,30 @@
     copy_all.wait()
     loads[1].wait()
 
-    def block_for(row):
-        return jnp.clip(lax.rem(asked_all[row, 0, me], 128) - 1, 0, 63)
-
-    def stage(i, carry):
-        block = pool[block_for(gathered_row(*shifted(i)))]
-        for c in range(KV_HEADS):
-            staged[c, i - 1, :, :HEAD_DIM] = block[:, c * HEAD_DIM : (c + 1) * HEAD_DIM]
-            staged[c, i - 1, :, HEAD_DIM:] = block[:, (8 + c) * HEAD_DIM : (9 + c) * HEAD_DIM]
+    def stage_one(i, carry):
+        lay(asked_all[gathered_row(*shifted(i)), 0, me], staged, staged_last, i - 1)
         return carry
 
-    lax.fori_loop(1, N_ALL, stage, 0)
-    block = pool[block_for(0)]
-    for c in range(KV_HEADS):
-        arrived[c, 127, :, :HEAD_DIM] = block[:, c * HEAD_DIM : (c + 1) * HEAD_DIM]
-        arrived[c, 127, :, HEAD_DIM:] = block[:, (8 + c) * HEAD_DIM : (9 + c) * HEAD_DIM]
+    lax.fori_loop(1, N_ALL, stage_one, 0)
 
     def send(c):
         def one(i, carry):
-            pltpu.make_async_remote_copy(
-                staged.at[c, i - 1],
-                arrived.at[c, i - 1],
-                send_sem.at[c],
-                recv_sem.at[c],
-                device_id=partner(i),
-                device_id_type=MESH,
-            ).start()
+            send_one(staged.at[c], arrived.at[c], c, i)
+            return carry
+
+        lax.fori_loop(1, N_ALL, one, 0)
+
+    def send_last(n):
+        def one(i, carry):
+            send_one(staged_last.at[n], arrived_last.at[n], last + n, i)
             return carry
 
         lax.fori_loop(1, N_ALL, one, 0)
 
     for c in range(AHEAD):
         send(c)
+
+    lay(asked_all[0, 0, me], arrived, arrived_last, 127)
 
     suffix = steps.shape[0]
     rows = lax.broadcasted_iota(jnp.int32, (suffix, suffix), 0)
@@ -279,49 +293,87 @@
     group = queries.shape[1] // (KV_HEADS * HEAD_DIM)
     scale = HEAD_DIM ** (-0.5)
 
+    def wait_for(sem, n, source, target):
+        slots = pl.ds(0, N_ALL - 1)
+        pltpu.make_async_copy(source.at[slots], target.at[slots], sem.at[n]).wait()
+
+    def columns_of(c, h):
+        return pl.ds(pl.multiple_of((c * group + h) * HEAD_DIM, HEAD_DIM), HEAD_DIM)
+
+    def own(c):
+        return (
+            new[:, pl.ds(pl.multiple_of(c * HEAD_DIM, HEAD_DIM), HEAD_DIM)],
+            new[:, pl.ds(pl.multiple_of((c + 8) * HEAD_DIM, HEAD_DIM), HEAD_DIM)],
+        )
+
+    def softmax(query, keys, keys_new):
+        old = dot(query, keys, ((1,), (1,))) * scale + bias[0:1]
+        fresh = jnp.where(lower, dot(query, keys_new, ((1,), (1,))) * scale, -1e30)
+        peak = jnp.maximum(
+            jnp.max(old, axis=1, keepdims=True), jnp.max(fresh, axis=1, keepdims=True)
+        )
+        old = jnp.exp(old - peak)
+        fresh = jnp.exp(fresh - peak)
+        return old, fresh, jnp.sum(old, axis=1, keepdims=True) + jnp.sum(fresh, axis=1, keepdims=True)
+
     def attend(c, carry):
-        pltpu.make_async_copy(
-            staged.at[c, 0 : N_ALL - 1], arrived.at[c, 0 : N_ALL - 1], recv_sem.at[c]
-        ).wait()
+        wait_for(recv_sem, c, staged.at[c], arrived.at[c])
         keys = arrived[c, :, :, :HEAD_DIM].reshape(N_ALL * BLK, HEAD_DIM)
         values = arrived[c, :, :, HEAD_DIM:].reshape(N_ALL * BLK, HEAD_DIM)
-        keys_new = new[:, pl.ds(pl.multiple_of(c * HEAD_DIM, HEAD_DIM), HEAD_DIM)]
-        values_new = new[:, pl.ds(pl.multiple_of((c + 8) * HEAD_DIM, HEAD_DIM), HEAD_DIM)]
+        keys_new, values_new = own(c)
 
         def one(h, carry):
-            columns = pl.ds(pl.multiple_of((c * group + h) * HEAD_DIM, HEAD_DIM), HEAD_DIM)
-            query = queries[:, columns]
-            old = dot(query, keys, ((1,), (1,))) * scale + bias[0:1]
-            fresh = jnp.where(lower, dot(query, keys_new, ((1,), (1,))) * scale, -1e30)
-            peak = jnp.maximum(
-                jnp.max(old, axis=1, keepdims=True), jnp.max(fresh, axis=1, keepdims=True)
-            )
-            old = jnp.exp(old - peak)
-            fresh = jnp.exp(fresh - peak)
-            weight = jnp.sum(old, axis=1, keepdims=True) + jnp.sum(fresh, axis=1, keepdims=True)
+            old, fresh, weight = softmax(queries[:, columns_of(c, h)], keys, keys_new)
             result = dot(old.astype(BF16), values) + dot(fresh.astype(BF16), values_new)
-            attended[:, columns] = (result / weight).astype(BF16)
+            attended[:, columns_of(c, h)] = (result / weight).astype(BF16)
             return carry
 
         lax.fori_loop(0, group, one, 0)
 
-        @pl.when(c + AHEAD < KV_HEADS)
+        @pl.when(c + AHEAD < last)
         def _():
             send(c + AHEAD)
 
+        @pl.when(c + AHEAD == last)
+        def _():
+            send_last(0)
+            send_last(1)
+
         return carry
 
-    lax.fori_loop(0, KV_HEADS, attend, 0)
+    lax.fori_loop(0, last, attend, 0)
+
+    keys_new, values_new = own(last)
+    wait_for(recv_sem, last, staged_last.at[0], arrived_last.at[0])
+    keys = arrived_last[0].reshape(N_ALL * BLK, HEAD_DIM)
+
+    def weigh(h, carry):
+        old, fresh, weight = softmax(queries[:, columns_of(last, h)], keys, keys_new)
+        weights[h] = jnp.broadcast_to(weight, (suffix, HEAD_DIM))
+        partial[h] = dot(fresh.astype(BF16), values_new)
+        rounded[h] = old.astype(BF16)
+        return carry
+
+    lax.fori_loop(0, group, weigh, 0)
+    wait_for(recv_sem, last + 1, staged_last.at[1], arrived_last.at[1])
+    values = arrived_last[1].reshape(N_ALL * BLK, HEAD_DIM)
+
+    def finish(h, carry):
+        result = dot(rounded[h], values) + partial[h]
+        attended[:, columns_of(last, h)] = (result / weights[h]).astype(BF16)
+        return carry
+
+    lax.fori_loop(0, group, finish, 0)
 
     pltpu.make_async_copy(asked.at[pl.ds(0, 7)], asked.at[pl.ds(1, 7)], ask_send_sem.at[0]).wait()
     pltpu.make_async_copy(
         asked.at[pl.ds(0, 120)], asked.at[pl.ds(8, 120)], ask_send_sem.at[1]
     ).wait()
     pltpu.make_async_copy(state_out, state_in.at[0:3], state_send_sem).wait()
-    for c in range(KV_HEADS):
-        pltpu.make_async_copy(
-            staged.at[c, 0 : N_ALL - 1], arrived.at[c, 0 : N_ALL - 1], send_sem.at[c]
-        ).wait()
+    for c in range(last):
+        wait_for(send_sem, c, staged.at[c], arrived.at[c])
+    for n in range(2):
+        wait_for(send_sem, last + n, staged_last.at[n], arrived_last.at[n])
 
 
 def body(
@@ -344,6 +396,7 @@
     n_all = lax.axis_size(("grp", "dev"))
     suffix, channels = ssm_input.shape
     heads = decay_rate.shape[0]
+    group = queries.shape[1] // (KV_HEADS * HEAD_DIM)
     states = state_in.shape[1]
     smem = pl.BlockSpec(memory_space=pltpu.SMEM)
     vmem = pl.BlockSpec(memory_space=pltpu.VMEM)
@@ -363,13 +416,17 @@
             pltpu.VMEM(queries.shape, BF16),
             pltpu.VMEM(new_kv.shape, BF16),
             pltpu.VMEM(ssm_input.shape, BF16),
-            pltpu.VMEM((KV_HEADS, n_all, BLK, 2 * HEAD_DIM), BF16),
-            pltpu.VMEM((KV_HEADS, n_all, BLK, 2 * HEAD_DIM), BF16),
+            pltpu.VMEM((KV_HEADS - 1, n_all, BLK, 2 * HEAD_DIM), BF16),
+            pltpu.VMEM((KV_HEADS - 1, n_all, BLK, 2 * HEAD_DIM), BF16),
+            pltpu.VMEM((2, n_all, BLK, HEAD_DIM), BF16),
+            pltpu.VMEM((2, n_all, BLK, HEAD_DIM), BF16),
             pltpu.VMEM((3, states, channels), BF16),
             pltpu.VMEM((4, states, channels), BF16),
             pltpu.VMEM((n_all, 1, n_all), jnp.int32),
-            pltpu.SMEM((8, 1, n_all), jnp.int32),
             pltpu.SMEM((n_all, 1, n_all), jnp.int32),
+            pltpu.VMEM((group, suffix, HEAD_DIM), F32),
+            pltpu.VMEM((group, suffix, HEAD_DIM), F32),
+            pltpu.VMEM((group, suffix, n_all * BLK), BF16),
             pltpu.VMEM((8, n_all * BLK), F32),
             pltpu.VMEM((suffix, 2 * heads), BF16),
             pltpu.VMEM((suffix, 2 * heads), BF16),
@@ -378,8 +435,8 @@
             pltpu.VMEM((suffix, suffix), BF16),
             pltpu.VMEM((2 * states, suffix), BF16),
             pltpu.SemaphoreType.DMA((5,)),
-            pltpu.SemaphoreType.DMA((KV_HEADS,)),
-            pltpu.SemaphoreType.DMA((KV_HEADS,)),
+            pltpu.SemaphoreType.DMA((KV_HEADS + 1,)),
+            pltpu.SemaphoreType.DMA((KV_HEADS + 1,)),
             pltpu.SemaphoreType.DMA,
             pltpu.SemaphoreType.DMA,
             pltpu.SemaphoreType.DMA((2,)),

time: 130 us -> 127 us (0.977)
  Pallas kernels: 124 us -> 120 us
    pallas_call x1, Pallas kernels: 124 us -> 120 us  [body(): pl.pallas_call(kernel, name='prefill', out_shape=(pltpu.VMEM(queries.shap...]
where the time goes in v2:
time: 127 us; the launch traced here: 126 us
  Pallas kernels  120 us (94%)
  local copies, waits for them, and re-layouts  3.33 us (3%)
  between operations  2.58 us (2%)
    pallas_call x1, Pallas kernels, body(): pl.pallas_call(kernel, name='prefill', out_shape=(pltpu.VMEM(queries.shap...  120 us
    unnamed x2, local copies, waits for them, and re-layouts  3.33 us

profile of v2, /device:TPU:1, one launch (start us, length us, event | category | flops | bytes accessed | tf_op | source)
XLA Modules:
  0.0 126.0 jit_solution(10160164993519667925)
XLA Ops:
  2.6 120.1 %prefill.1 = (bf16[256,4096]{1,0:T(8,128)(2,1)S(1)}, bf16[256,8192]{1,0:T(8,128)(2,1)S(1)}) custom-call(s32[1]{0:T(128)S(6)} %copy.22.state_group, s32[1]{0:T(128)S(6)} %copy.23.state_slot, s32[1]{0:T(128)S(6)} %copy.21.hit_count, s32[1,96]{1,0:T(1,128)} %hit_holder.1, s32[1,96]{1,0:T(1,128)} %hit_block.1, f32[256,128]{1,0:T(8,128)} %steps.1, ...), custom_call_target="tpu_custom_call" | custom-call | tf_op jit(solution)/shard_map/prefill/pallas_call | solution.py:404
  122.7 1.3 %copy.19 = bf16[256,4096]{1,0:T(8,128)(2,1)} copy(bf16[256,4096]{1,0:T(8,128)(2,1)S(1)} %get-tuple-element.2) | data formatting | bytes 4194304
  124.0 2.0 %copy.20 = bf16[256,8192]{1,0:T(8,128)(2,1)} copy(bf16[256,8192]{1,0:T(8,128)(2,1)S(1)} %get-tuple-element.3) | data formatting | bytes 8388608
